TPU v7x, 128 devices: a whole 4x4x4 slice. The times are simulated.
128 devices in a mesh: lon: 16 (over y_lo, x, core), lat: 8 (over z, y_hi).
Axes of the slice: x: 4, y: 4 (y_hi: 2, y_lo: 2; y = y_hi * 2 + y_lo), z: 4, core: 2. Of those that a mesh axis runs over, the one named last changes fastest.
Arguments:
- terminal_error_derivative: float32 [4, 48, 512, 2048], P(None, None, 'lat', 'lon'), may hold values from -6 to 6
- trajectory_advective_shift: float32 [2, 2, 48, 512, 2048], P(None, None, None, 'lat', 'lon'), may hold values from -1 to 1
- layer_interaction_matrix: float32 [48, 4, 4], replicated, may hold values from -1.2 to 1.2
- measured_local_profile_slot: int32 [128, 16, 256], P(('lon', 'lat')), may hold values from 0 to 8191
- measured_active_tally: int32 [128, 16], P(('lon', 'lat')), may hold values from 0 to 256, as said below
- measurement_operator_matrix: bfloat16 [128, 16, 192, 256], P(('lon', 'lat')), may hold values from -0.4375 to 0.4375
- measured_departure_values: float32 [128, 16, 256], P(('lon', 'lat')), may hold values from -5 to 5
Outputs:
- analysis_sens: float32 [4, 48, 512, 2048], P(None, None, 'lat', 'lon')
- obs_impact: float32 [128, 16, 256], P(('lon', 'lat'))
Inputs may be any that keep to these rules, and one draw needn't show every extreme that they name: `measured_active_tally`: entry [s, k] counts the live slots of device s's list for sector k; slots from it on are padding. In every draw some list is full with 256 entries.
All inputs are finite; a program needn't handle non-finite values.
Results may differ from a plain program's by a relative error of at most 0.0005.
Values may be sent and summed in bfloat16 or wider, within the bound.
A program may use at most 192 MiB of HBM per device.

v0:
```python
import jax
import jax.numpy as jnp
from jax import lax
from jax.sharding import PartitionSpec as P


def extended(cells, sides, width, closed):
    for axis, dim in sides:
        count = lax.axis_size(axis)
        ends = count if closed else count - 1
        head = lax.slice_in_dim(cells, 0, width, axis=dim)
        tail = lax.slice_in_dim(cells, cells.shape[dim] - width, cells.shape[dim], axis=dim)
        cells = jnp.concatenate(
            [
                lax.ppermute(tail, axis, [(i, (i + 1) % count) for i in range(ends)]),
                cells,
                lax.ppermute(head, axis, [((i + 1) % count, i) for i in range(ends)]),
            ],
            axis=dim,
        )
    return cells


def couple(prognostic_variable_slot, layer_interaction_matrix):
    return jnp.einsum(
        "lef,elab->flab",
        layer_interaction_matrix,
        prognostic_variable_slot,
        precision=lax.Precision.HIGHEST,
    )


def neighbour_terms(product, rim, axis):
    length = product.shape[axis]
    position = lax.broadcasted_iota(jnp.int32, product.shape, axis)
    lower_rim = lax.slice_in_dim(rim, 0, 1, axis=axis)
    upper_rim = lax.slice_in_dim(rim, 3, 4, axis=axis)
    from_lower = jnp.where(position == 0, lower_rim, jnp.roll(product, 1, axis=axis))
    from_upper = jnp.where(position == length - 1, upper_rim, jnp.roll(product, -1, axis=axis))
    return from_lower - from_upper


def on_device(
    terminal_error_derivative,
    trajectory_advective_shift,
    layer_interaction_matrix,
    measured_local_profile_slot,
    measured_active_tally,
    measurement_operator_matrix,
    measured_departure_values,
):
    sectors = measured_local_profile_slot.shape[1]
    slots = measured_local_profile_slot.shape[2]
    wanted = lax.all_to_all(
        measured_local_profile_slot[0], "lon", split_axis=0, concat_axis=0, tiled=True
    )
    prognostic_variable_slot = terminal_error_derivative
    for step in (1, 0):
        lon_prod = trajectory_advective_shift[step, 0][None] * prognostic_variable_slot
        lat_prod = trajectory_advective_shift[step, 1][None] * prognostic_variable_slot
        lon_edges = jnp.concatenate([lon_prod[..., :1], lon_prod[..., -1:]], axis=3)
        lat_edges = jnp.concatenate([lat_prod[:, :, :1], lat_prod[:, :, -1:]], axis=2)
        lon_cycle = extended(lon_edges.astype(jnp.bfloat16), (("lon", 3),), 1, True).astype(
            lon_edges.dtype
        )
        lat_cycle = extended(lat_edges.astype(jnp.bfloat16), (("lat", 2),), 1, False).astype(
            lat_edges.dtype
        )
        lon_term = neighbour_terms(lon_prod, lon_cycle, 3)
        lat_term = neighbour_terms(lat_prod, lat_cycle, 2)
        prognostic_variable_slot = (
            prognostic_variable_slot
            + couple(prognostic_variable_slot, layer_interaction_matrix)
            - lon_term
            - lat_term
        )
    flat = prognostic_variable_slot.reshape(
        prognostic_variable_slot.shape[0] * prognostic_variable_slot.shape[1], -1
    )
    picked = flat[:, wanted]
    returned = lax.all_to_all(picked, "lon", split_axis=1, concat_axis=1, tiled=True)
    sens = jnp.sum(
        measurement_operator_matrix[0].astype(jnp.float32) * jnp.swapaxes(returned, 0, 1), axis=1
    )
    live = lax.broadcasted_iota(jnp.int32, (sectors, slots), 1) < measured_active_tally[0][:, None]
    obs_impact = jnp.where(live, measured_departure_values[0] * sens, jnp.float32(0.0))[None]
    return (prognostic_variable_slot, obs_impact)


def solution(mesh):
    in_specs = (
        P(None, None, "lat", "lon"),
        P(None, None, None, "lat", "lon"),
        P(),
        P(("lon", "lat"), None, None),
        P(("lon", "lat"), None),
        P(("lon", "lat"), None, None, None),
        P(("lon", "lat"), None, None),
    )
    out_specs = (P(None, None, "lat", "lon"), P(("lon", "lat"), None, None))
    return jax.shard_map(
        on_device, mesh=mesh, in_specs=in_specs, out_specs=out_specs, check_vma=False
    )
```

profile of v0, /device:TPU:1, one launch (start us, length us, event | category | flops | bytes accessed | tf_op | source)
XLA Modules:
  0.0 466.5 jit_solution(5339470776129367898)
XLA Ops:
  6.1 9.0 %copy_multiply_fusion.1 = (f32[4,48,64,128]{3,0,2,1:T(4,128)S(1)}, f32[4,48,64,128]{3,0,2,1:T(4,128)}) fusion(f32[4,48,64,128]{3,2,1,0:T(8,128)S(1)} %copy-done.3, f32[48,64,128]{2,1,0:T(8,128)S(1)} %get-tuple-element.28, f32[48,64,128]{2,1,0:T(8,128)S(1)} %get-tuple-element.27), kind=kLoop, calls=%fused_computation.21 | loop fusion | flops 3145728 | bytes 22020096 | tf_op jit(solution)/shard_map/mul | solution.py:59
  39.6 6.6 %all-to-all-start = ((s32[16,1,256]{2,1,0:T(1,128)}), s32[16,1,256]{2,1,0:T(1,128)S(1)}, u32[]{:S(2)}, u32[]{:S(2)}) async-start(s32[16,1,256]{2,1,0:T(1,128)} %all_to_all.11), calls=%async_computation | async-start | bytes 32768 | tf_op jit(solution)/shard_map/all_to_all | solution.py:54
  46.2 12.6 %fusion.21 = (f32[4,48,64,1]{3,0,2,1:T(4,128)}, f32[4,48,64,1]{3,0,2,1:T(4,128)}) fusion(f32[4,48,64,128]{3,0,2,1:T(4,128)} %copy-done), kind=kLoop, calls=%fused_computation.69 | loop fusion | bytes 196608 | tf_op jit(solution)/shard_map/slice | solution.py:61
  58.8 12.6 %fusion.22 = (f32[4,48,64,127]{3,0,2,1:T(4,128)}, f32[4,48,64,127]{3,0,2,1:T(4,128)}) fusion(f32[4,48,64,128]{3,0,2,1:T(4,128)} %copy-done), kind=kLoop, calls=%fused_computation.70 | loop fusion | bytes 24969216 | tf_op jit(solution)/shard_map/jit(_roll_static)/slice | solution.py:38
  71.3 9.8 %fusion.25 = (f32[4,48,63,128]{3,0,2,1:T(4,128)}, f32[4,48,63,128]{3,0,2,1:T(4,128)}) fusion(f32[4,48,64,128]{3,0,2,1:T(4,128)} %get-tuple-element.39), kind=kLoop, calls=%fused_computation.73 | loop fusion | bytes 24772608 | tf_op jit(solution)/shard_map/jit(_roll_static)/slice | solution.py:38
  94.3 12.6 %maximum_convert_fusion = f32[4,48,64,4]{3,0,2,1:T(4,128)} fusion(bf16[4,48,64,1]{3,0,2,1:T(4,128)(2,1)} %copy.66, bf16[4,48,64,1]{3,0,2,1:T(4,128)(2,1)S(1)} %get-tuple-element.36, bf16[4,48,64,1]{3,0,2,1:T(4,128)(2,1)} %get-tuple-element.37, bf16[4,48,64,1]{3,0,2,1:T(4,128)(2,1)} %copy.65), kind=kLoop, calls=%fused_computation.24 | loop fusion | flops 393216 | bytes 294912 | tf_op jit(solution)/shard_map/convert_element_type | solution.py:63
  107.0 12.8 %fusion.20 = (f32[4,48,64,1]{3,0,2,1:T(4,128)}, f32[4,48,64,1]{3,0,2,1:T(4,128)}) fusion(f32[4,48,64,4]{3,0,2,1:T(4,128)} %maximum_convert_fusion), kind=kLoop, calls=%fused_computation.68 | loop fusion | bytes 196608 | tf_op jit(solution)/shard_map/slice | solution.py:36
  119.8 21.2 %copy.89 = f32[4,48,64,1]{0,2,1,3:T(8,128)} copy(f32[4,48,64,1]{3,0,2,1:T(4,128)} %get-tuple-element.30) | data formatting | bytes 98304 | tf_op jit(solution)/shard_map/jit(_where)/broadcast_in_dim | solution.py:38
  141.0 21.1 %copy.90 = f32[4,48,64,1]{0,2,1,3:T(8,128)} copy(f32[4,48,64,1]{3,0,2,1:T(4,128)} %get-tuple-element.31) | data formatting | bytes 98304 | tf_op jit(solution)/shard_map/jit(_where)/broadcast_in_dim | solution.py:39
  163.1 38.3 %broadcast_multiply_fusion = (f32[4,48,64,128]{3,0,2,1:T(4,128)}, f32[4,48,64,128]{3,0,2,1:T(4,128)}) fusion(f32[48,64,128]{2,1,0:T(8,128)S(1)} %copy-done.4, f32[4,48,1,128]{3,0,2,1:T(4,128)S(1)} %get-tuple-element.41, f32[4,48,63,128]{3,0,2,1:T(4,128)} %get-tuple-element.43, f32[4,48,128]{2,0,1:T(4,128)S(1)} %get-tuple-element.49, ...), kind=kOutput, calls=%fused_computation.28 | convolution fusion | flops 97517568 | bytes 45911424 | tf_op jit(solution)/shard_map/lef,elab->flab/dot_general | solution.py:25
  201.4 8.3 %broadcast_multiply_fusion.1 = f32[4,48,64,128]{3,0,2,1:T(4,128)} fusion(f32[4,48,64,128]{3,0,2,1:T(4,128)} %get-tuple-element.11, f32[48,64,128]{2,1,0:T(8,128)S(1)} %copy-done.2), kind=kLoop, calls=%fused_computation.29 | loop fusion | flops 1572864 | bytes 14155776 | tf_op jit(solution)/shard_map/mul | solution.py:59
  209.8 9.5 %fusion.14 = (bf16[4,48,64,1]{3,0,2,1:T(4,128)(2,1)S(1)}, bf16[4,48,64,1]{3,0,2,1:T(4,128)(2,1)}) fusion(f32[4,48,64,128]{3,0,2,1:T(4,128)} %broadcast_multiply_fusion.1), kind=kLoop, calls=%fused_computation.62 | loop fusion | bytes 98304 | tf_op jit(solution)/shard_map/slice | solution.py:61
  219.3 12.8 %fusion.18 = (f32[4,48,64,127]{3,0,2,1:T(4,128)}, f32[4,48,64,127]{3,0,2,1:T(4,128)}) fusion(f32[4,48,64,128]{3,0,2,1:T(4,128)} %broadcast_multiply_fusion.1), kind=kLoop, calls=%fused_computation.66 | loop fusion | bytes 24969216 | tf_op jit(solution)/shard_map/jit(_roll_static)/slice | solution.py:39
  232.1 12.8 %fusion.19 = (f32[4,48,64,1]{3,0,2,1:T(4,128)}, f32[4,48,64,1]{3,0,2,1:T(4,128)}) fusion(f32[4,48,64,128]{3,0,2,1:T(4,128)} %broadcast_multiply_fusion.1), kind=kLoop, calls=%fused_computation.67 | loop fusion | bytes 196608 | tf_op jit(solution)/shard_map/slice | solution.py:61
  245.0 9.8 %fusion.16 = (f32[4,48,63,128]{3,0,2,1:T(4,128)}, f32[4,48,63,128]{3,0,2,1:T(4,128)}) fusion(f32[4,48,64,128]{3,0,2,1:T(4,128)} %get-tuple-element.10), kind=kLoop, calls=%fused_computation.64 | loop fusion | bytes 24772608 | tf_op jit(solution)/shard_map/jit(_roll_static)/slice | solution.py:39
  284.9 12.4 %maximum_convert_fusion.1 = f32[4,48,64,4]{3,0,2,1:T(4,128)} fusion(bf16[4,48,64,1]{3,0,2,1:T(4,128)(2,1)} %copy.76, bf16[4,48,64,1]{3,0,2,1:T(4,128)(2,1)S(1)} %get-tuple-element.14, bf16[4,48,64,1]{3,0,2,1:T(4,128)(2,1)} %get-tuple-element.15, bf16[4,48,64,1]{3,0,2,1:T(4,128)(2,1)} %copy.75), kind=kLoop, calls=%fused_computation.25 | loop fusion | flops 393216 | bytes 294912 | tf_op jit(solution)/shard_map/convert_element_type | solution.py:63
  297.3 12.7 %fusion.13 = (f32[4,48,64,1]{3,0,2,1:T(4,128)}, f32[4,48,64,1]{3,0,2,1:T(4,128)}) fusion(f32[4,48,64,4]{3,0,2,1:T(4,128)} %maximum_convert_fusion.1), kind=kLoop, calls=%fused_computation.61 | loop fusion | bytes 196608 | tf_op jit(solution)/shard_map/slice | solution.py:36
  309.9 20.9 %copy.93 = f32[4,48,64,1]{0,2,1,3:T(8,128)S(1)} copy(f32[4,48,64,1]{3,0,2,1:T(4,128)} %get-tuple-element.12) | data formatting | bytes 98304 | tf_op jit(solution)/shard_map/jit(_where)/broadcast_in_dim | solution.py:38
  330.8 20.9 %copy.94 = f32[4,48,64,1]{0,2,1,3:T(8,128)S(1)} copy(f32[4,48,64,1]{3,0,2,1:T(4,128)} %get-tuple-element.13) | data formatting | bytes 98304 | tf_op jit(solution)/shard_map/jit(_where)/broadcast_in_dim | solution.py:39
  352.7 27.7 %fusion.6 = f32[4,48,64,128]{3,0,2,1:T(4,128)S(1)} fusion(f32[4,48,64,127]{3,0,2,1:T(4,128)} %get-tuple-element.23, f32[4,48,64,1]{3,0,2,1:T(4,128)} %get-tuple-element.25, f32[4,48,64,1]{3,0,2,1:T(4,128)} %get-tuple-element.24, f32[4,48,64,127]{3,0,2,1:T(4,128)} %get-tuple-element.22, f32[4,48,63,128]{3,0,2,1:T(4,128)} %get-tuple-element.19, ...), kind=kOutput, calls=%fused_computation.13 | convolution fusion | flops 95944704 | bytes 38047104 | tf_op jit(solution)/shard_map/lef,elab->flab/dot_general | solution.py:25
  381.3 8.3 %copy.105 = f32[24,8,64,128]{3,1,2,0:T(8,128)} copy(f32[24,8,64,128]{3,2,1,0:T(8,128)S(1)} %bitcast.58) | data formatting | bytes 12582912
  389.6 8.6 %copy.82 = f32[192,8192]{0,1:T(8,128)} copy(f32[192,8192]{1,0:T(8,128)} %bitcast.59) | data formatting | bytes 12582912 | tf_op jit(solution)/shard_map/reshape | solution.py:77
  398.1 19.5 %gather_fusion = f32[4096,192]{1,0:T(8,128)} fusion(f32[192,8192]{0,1:T(8,128)} %copy.82, s32[4096]{0:T(1024)S(1)} %copy-done.6), kind=kCustom, calls=%fused_computation | custom fusion | bytes 6307840 | tf_op jit(solution)/shard_map/gather | solution.py:80
  421.5 43.5 %all_to_all.17 = f32[192,16,256]{2,0,1:T(8,128)S(1)} all-to-all(f32[192,16,256]{2,0,1:T(8,128)S(1)} %bitcast.61), channel_id=1, replica_groups=mesh['lon'=16,'lat'=8] {'lon'}, dimensions={1} | all-to-all | bytes 6291456 | tf_op jit(solution)/shard_map/all_to_all | solution.py:81
  (71 shorter events, 80.7 us)
Async XLA Ops:
  0.6 5.5 %copy-start.3 = (f32[4,48,64,128]{3,2,1,0:T(8,128)S(1)}, f32[4,48,64,128]{3,2,1,0:T(8,128)}, u32[]{:S(2)}) copy-start(f32[4,48,64,128]{3,2,1,0:T(8,128)} %param.7) | copy-start | bytes 18874372
  15.1 4.6 copy-start
  19.7 19.2 %copy-start.8 = (s32[1,16,256]{2,1,0:T(8,128)S(1)}, s32[1,16,256]{2,1,0:T(8,128)}, u32[]{:S(2)}) copy-start(s32[1,16,256]{2,1,0:T(8,128)} %param.10) | copy-start | bytes 49156
  23.0 61.8 %collective-permute-start = (bf16[4,48,64,1]{2,1,3,0:T(8,128)(2,1)}, bf16[4,48,64,1]{2,1,3,0:T(8,128)(2,1)}, u32[]{:S(2)}, u32[]{:S(2)}) collective-permute-start(bf16[4,48,64,1]{2,1,3,0:T(8,128)(2,1)} %copy.63), channel_id=1, source_target_pairs={{0,8},{8,16},{16,24},{24,32},{32,40},{40,48},{48,56},{56,64},{64,7... | collective-permute-start | bytes 73736 | tf_op jit(solution)/shard_map/ppermute | solution.py:15
  31.2 58.3 %collective-permute-start.1 = (bf16[4,48,64,1]{2,1,3,0:T(8,128)(2,1)}, bf16[4,48,64,1]{2,1,3,0:T(8,128)(2,1)}, u32[]{:S(2)}, u32[]{:S(2)}) collective-permute-start(bf16[4,48,64,1]{2,1,3,0:T(8,128)(2,1)} %copy.64), channel_id=1, source_target_pairs={{8,0},{16,8},{24,16},{32,24},{40,32},{48,40},{56,48},{64,56},{72,6... | collective-permute-start | bytes 73736 | tf_op jit(solution)/shard_map/ppermute | solution.py:17
  32.2 130.0 %collective-permute-start.2 = (bf16[4,48,1,128]{3,0,2,1:T(4,128)(2,1)S(1)}, bf16[4,48,1,128]{3,0,2,1:T(4,128)(2,1)}, u32[]{:S(2)}, u32[]{:S(2)}) collective-permute-start(bf16[4,48,1,128]{3,0,2,1:T(4,128)(2,1)S(1)} %get-tuple-element.44), channel_id=1, source_target_pairs={{0,1},{1,2},{2,3},{3,4},{4,5},{5,6},{6,7},{8,9},{9,10},{10,11},{11... | collective-permute-start | bytes 147464 | tf_op jit(solution)/shard_map/ppermute | solution.py:15
  37.6 124.5 %collective-permute-start.3 = (bf16[4,48,1,128]{3,0,2,1:T(4,128)(2,1)S(1)}, bf16[4,48,1,128]{3,0,2,1:T(4,128)(2,1)}, u32[]{:S(2)}, u32[]{:S(2)}) collective-permute-start(bf16[4,48,1,128]{3,0,2,1:T(4,128)(2,1)S(1)} %get-tuple-element.45), channel_id=1, source_target_pairs={{1,0},{2,1},{3,2},{4,3},{5,4},{6,5},{7,6},{9,8},{10,9},{11,10},{12... | collective-permute-start | bytes 147464 | tf_op jit(solution)/shard_map/ppermute | solution.py:17
  39.6 44.6 %all-to-all-start = ((s32[16,1,256]{2,1,0:T(1,128)}), s32[16,1,256]{2,1,0:T(1,128)S(1)}, u32[]{:S(2)}, u32[]{:S(2)}) async-start(s32[16,1,256]{2,1,0:T(1,128)} %all_to_all.11), calls=%async_computation | async-start | bytes 32768 | tf_op jit(solution)/shard_map/all_to_all | solution.py:54
  119.7 43.3 %copy-start.4 = (f32[48,64,128]{2,1,0:T(8,128)S(1)}, f32[48,64,128]{2,1,0:T(8,128)}, u32[]{:S(2)}) copy-start(f32[48,64,128]{2,1,0:T(8,128)} %get-tuple-element.29) | copy-start | bytes 4718596
  119.7 43.3 %copy-start.10 = (pred[64]{0:T(512)(128)(4,1)S(1)}, pred[64]{0:T(512)(128)(4,1)}, u32[]{:S(2)}) copy-start(pred[64]{0:T(512)(128)(4,1)} %get-tuple-element.50) | copy-start | bytes 196
  119.7 43.3 %copy-start.11 = (pred[64]{0:T(512)(128)(4,1)S(1)}, pred[64]{0:T(512)(128)(4,1)}, u32[]{:S(2)}) copy-start(pred[64]{0:T(512)(128)(4,1)} %get-tuple-element.51) | copy-start | bytes 196
  119.7 43.3 %copy-start.12 = (pred[128]{0:T(512)(128)(4,1)S(1)}, pred[128]{0:T(512)(128)(4,1)}, u32[]{:S(2)}) copy-start(pred[128]{0:T(512)(128)(4,1)} %get-tuple-element.52) | copy-start | bytes 388
  119.8 43.3 %copy-start.13 = (pred[128]{0:T(512)(128)(4,1)S(1)}, pred[128]{0:T(512)(128)(4,1)}, u32[]{:S(2)}) copy-start(pred[128]{0:T(512)(128)(4,1)} %get-tuple-element.53) | copy-start | bytes 388
  163.1 38.3 %copy-start.2 = (f32[48,64,128]{2,1,0:T(8,128)S(1)}, f32[48,64,128]{2,1,0:T(8,128)}, u32[]{:S(2)}) copy-start(f32[48,64,128]{2,1,0:T(8,128)} %get-tuple-element.26) | copy-start | bytes 4718596
  259.0 15.9 %collective-permute-start.4 = (bf16[4,48,64,1]{2,1,3,0:T(8,128)(2,1)}, bf16[4,48,64,1]{2,1,3,0:T(8,128)(2,1)}, u32[]{:S(2)}, u32[]{:S(2)}) collective-permute-start(bf16[4,48,64,1]{2,1,3,0:T(8,128)(2,1)} %copy.73), channel_id=1, source_target_pairs={{0,8},{8,16},{16,24},{24,32},{32,40},{40,48},{48,56},{56,64},{64,7... | collective-permute-start | bytes 73736 | tf_op jit(solution)/shard_map/ppermute | solution.py:15
  266.3 13.7 %collective-permute-start.5 = (bf16[4,48,64,1]{2,1,3,0:T(8,128)(2,1)}, bf16[4,48,64,1]{2,1,3,0:T(8,128)(2,1)}, u32[]{:S(2)}, u32[]{:S(2)}) collective-permute-start(bf16[4,48,64,1]{2,1,3,0:T(8,128)(2,1)} %copy.74), channel_id=1, source_target_pairs={{8,0},{16,8},{24,16},{32,24},{40,32},{48,40},{56,48},{64,56},{72,6... | collective-permute-start | bytes 73736 | tf_op jit(solution)/shard_map/ppermute | solution.py:17
  267.3 84.5 %collective-permute-start.6 = (bf16[4,48,1,128]{3,0,2,1:T(4,128)(2,1)S(1)}, bf16[4,48,1,128]{3,0,2,1:T(4,128)(2,1)}, u32[]{:S(2)}, u32[]{:S(2)}) collective-permute-start(bf16[4,48,1,128]{3,0,2,1:T(4,128)(2,1)S(1)} %get-tuple-element.16), channel_id=1, source_target_pairs={{0,1},{1,2},{2,3},{3,4},{4,5},{5,6},{6,7},{8,9},{9,10},{10,11},{11... | collective-permute-start | bytes 147464 | tf_op jit(solution)/shard_map/ppermute | solution.py:15
  273.7 78.1 %collective-permute-start.7 = (bf16[4,48,1,128]{3,0,2,1:T(4,128)(2,1)S(1)}, bf16[4,48,1,128]{3,0,2,1:T(4,128)(2,1)}, u32[]{:S(2)}, u32[]{:S(2)}) collective-permute-start(bf16[4,48,1,128]{3,0,2,1:T(4,128)(2,1)S(1)} %get-tuple-element.17), channel_id=1, source_target_pairs={{1,0},{2,1},{3,2},{4,3},{5,4},{6,5},{7,6},{9,8},{10,9},{11,10},{12... | collective-permute-start | bytes 147464 | tf_op jit(solution)/shard_map/ppermute | solution.py:17
  381.3 8.3 %copy-start.1 = (f32[4,48,64,128]{3,2,1,0:T(8,128)}, f32[4,48,64,128]{3,2,1,0:T(8,128)S(1)}, u32[]{:S(2)}) copy-start(f32[4,48,64,128]{3,2,1,0:T(8,128)S(1)} %copy.84) | copy-start | bytes 18874372
  389.6 8.6 %copy-start.6 = (s32[4096]{0:T(1024)S(1)}, s32[4096]{0:T(1024)}, u32[]{:S(2)}) copy-start(s32[4096]{0:T(1024)} %broadcast_clamp_fusion) | copy-start | bytes 49156
  421.5 43.5 %copy-start.5 = (bf16[1,16,192,256]{3,2,1,0:T(8,128)(2,1)S(1)}, bf16[1,16,192,256]{3,2,1,0:T(8,128)(2,1)}, u32[]{:S(2)}) copy-start(bf16[1,16,192,256]{3,2,1,0:T(8,128)(2,1)} %param.12) | copy-start | bytes 4718596
  421.5 43.9 %copy-start.7 = (f32[1,16,256]{2,1,0:T(8,128)S(1)}, f32[1,16,256]{2,1,0:T(8,128)}, u32[]{:S(2)}) copy-start(f32[1,16,256]{2,1,0:T(8,128)} %param.13) | copy-start | bytes 49156
  421.5 43.9 %copy-start.9 = (s32[1,16]{1,0:T(1,128)S(1)}, s32[1,16]{1,0:T(1,128)}, u32[]{:S(2)}) copy-start(s32[1,16]{1,0:T(1,128)} %param.11) | copy-start | bytes 196
where the time goes:
time: 475 us; the launch traced here: 466 us
  local copies, waits for them, and re-layouts  283 us (60%)
  matrix products  66 us (14%)
  other arithmetic  47 us (10%)
  blocking collectives  43.5 us (9%)
  starting transfers between devices  25.2 us (5%)
    dot_general x2, matrix products, couple(): jnp.einsum('lef,elab->flab', layer_interaction_matrix, prognostic_variabl...  66 us
    all_to_all x1, blocking collectives, on_device(): lax.all_to_all(picked, 'lon', split_axis=1, concat_axis=1, tiled=True)  43.5 us
    broadcast_in_dim x2, local copies, waits for them, and re-layouts, neighbour_terms(): jnp.where(position == 0, lower_rim, jnp.roll(product, 1, axis=axis))  42.2 us
    broadcast_in_dim x2, local copies, waits for them, and re-layouts, neighbour_terms(): jnp.where(position == length - 1, upper_rim, jnp.roll(product, -1, axis=a...  42.1 us
    slice x4, local copies, waits for them, and re-layouts, on_device(): lon_edges = jnp.concatenate([lon_prod[..., :1], lon_prod[..., -1:]], axis=3)  39.5 us
    slice x2, local copies, waits for them, and re-layouts, neighbour_terms(): lower_rim = lax.slice_in_dim(rim, 0, 1, axis=axis)  25.4 us
    convert_element_type x2, other arithmetic, on_device(): extended(lon_edges.astype(jnp.bfloat16), (('lon', 3),), 1, True)  25 us
    gather x2, local copies, waits for them, and re-layouts, on_device(): picked = flat[:, wanted]  23.3 us
  transfers between devices with their start and end apart: 9, of which 0 were waited for; matrix products, arithmetic and copies ran while one was open for 44% of the time, Pallas kernels for 0%

commit v1 on v0

v1 whole, which is shorter than its diff:
```python
import functools

import jax
import jax.numpy as jnp
from jax import lax
from jax.experimental import pallas as pl
from jax.experimental.pallas import tpu as pltpu
from jax.sharding import PartitionSpec as P

MESH = pl.DeviceIdType.MESH
F32 = jnp.float32
BF16 = jnp.bfloat16
CH = 16
SUB = 8


def each(lo, hi, body, unroll=1):
    def step(i, carry):
        body(i)
        return carry

    lax.fori_loop(lo, hi, step, 0, unroll=unroll)


def kernel(
    dims,
    g_ref, wind_ref, lim_ref, slot_ref, m_ref,
    a_ref, s_ref,
    cells, winds, coef, columns, m_in, slot_in, slot_sm, picked, eye2,
    lon_out, lon_in, lat_out, lat_in, edge, ring, halo, sens, sens_in,
    g_sem, w_sem, a_sem, m_send, m_recv, slot_send, slot_recv, local_sem,
    lon_send, lon_recv, lat_send, lat_recv, sens_send, sens_recv,
):
    n_lon, n_lat, fields, levels, rows, lanes, slots = dims
    chunks = levels // CH
    chan = fields * levels
    lon = lax.axis_index("lon")
    lat = lax.axis_index("lat")
    east, west = lax.rem(lon + 1, n_lon), lax.rem(lon + n_lon - 1, n_lon)
    north, south = lax.rem(lat + 1, n_lat), lax.rem(lat + n_lat - 1, n_lat)

    def fetch_first(l):
        c = l // CH
        for f in range(fields):
            pltpu.make_async_copy(
                g_ref.at[f, l], cells.at[:, f * levels + l, :], g_sem.at[c, f]
            ).start()
        for k in range(2):
            pltpu.make_async_copy(
                wind_ref.at[1, k, l], winds.at[k, :, l, :], w_sem.at[c, k]
            ).start()

    def fetch_second(l):
        c = l // CH
        for k in range(2):
            pltpu.make_async_copy(
                wind_ref.at[0, k, l], winds.at[2 + k, :, l, :], w_sem.at[c, 2 + k]
            ).start()

    each(0, levels, fetch_first)
    each(0, levels, fetch_second)

    def wait_g(c):
        for f in range(fields):
            block = cells.at[:, pl.ds(f * levels + c * CH, CH), :]
            pltpu.make_async_copy(block, block, g_sem.at[c, f]).wait()

    def wait_w(c, k):
        block = winds.at[k, :, pl.ds(c * CH, CH), :]
        pltpu.make_async_copy(block, block, w_sem.at[c, k]).wait()

    barrier = pltpu.get_barrier_semaphore()

    def greet(d):
        pl.semaphore_signal(
            barrier, inc=1, device_id={"lon": lax.rem(lon + d, n_lon)}, device_id_type=MESH
        )

    each(1, n_lon, greet)
    for other in (north, south):
        pl.semaphore_signal(barrier, inc=1, device_id={"lat": other}, device_id_type=MESH)
    pl.semaphore_wait(barrier, n_lon - 1 + 2)

    def slot_copy(d):
        peer = lax.rem(lon + d, n_lon)
        return pltpu.make_async_remote_copy(
            src_ref=slot_ref.at[0, pl.ds(peer, 1), :], dst_ref=slot_in.at[d],
            send_sem=slot_send.at[d], recv_sem=slot_recv.at[d],
            device_id={"lon": peer}, device_id_type=MESH,
        )

    def m_copy(d):
        peer = lax.rem(lon + d, n_lon)
        return pltpu.make_async_remote_copy(
            src_ref=m_ref.at[0, peer], dst_ref=m_in.at[d],
            send_sem=m_send.at[d], recv_sem=m_recv.at[d],
            device_id={"lon": peer}, device_id_type=MESH,
        )

    own_slot = pltpu.make_async_copy(
        slot_ref.at[0, pl.ds(lon, 1), :], slot_in.at[0], slot_recv.at[0]
    )
    own_m = pltpu.make_async_copy(m_ref.at[0, lon], m_in.at[0], m_recv.at[0])
    each(1, n_lon, lambda d: slot_copy(d).start())
    own_slot.start()

    def lon_copy(t, c, side):
        return pltpu.make_async_remote_copy(
            src_ref=lon_out.at[t, c], dst_ref=lon_in.at[t, c, side],
            send_sem=lon_send.at[t, c, side], recv_sem=lon_recv.at[t, c, side],
            device_id={"lon": east if side == 0 else west}, device_id_type=MESH,
        )

    def lat_copy(t, c, side):
        return pltpu.make_async_remote_copy(
            src_ref=lat_out.at[t, c, side], dst_ref=lat_in.at[t, c, side],
            send_sem=lat_send.at[t, c, side], recv_sem=lat_recv.at[t, c, side],
            device_id={"lat": north if side == 0 else south}, device_id_type=MESH,
        )

    lane = lax.broadcasted_iota(jnp.int32, (SUB, lanes), 1)
    pair = lane // 2

    def at(f, low):
        return pl.ds(pl.multiple_of(f * levels + low, SUB), SUB)

    def send_edges(t, c):
        lon_out[t, c] = edge[...].astype(BF16)
        for side, row in ((0, rows - 1), (1, 0)):
            w = winds[2 * t + 1, row, pl.ds(c * CH, CH), :]
            for f in range(fields):
                lat_out[t, c, side, f] = (
                    w * cells[row, pl.ds(f * levels + c * CH, CH), :]
                ).astype(BF16)
        for side in range(2):
            lon_copy(t, c, side).start()
            lat_copy(t, c, side).start()

    def first_edges(c):
        wait_g(c)
        wait_w(c, 0)
        wait_w(c, 1)

        def sub(h):
            low = pl.multiple_of(c * CH + h * SUB, SUB)

            def row(i, acc):
                u = winds[0, i, pl.ds(low, SUB), :]
                here = pair == i
                return tuple(
                    jnp.where(here, pltpu.roll(u * cells[i, at(f, low), :], 2 * i + 1, 1), acc[f])
                    for f in range(fields)
                )

            acc = lax.fori_loop(
                0, rows, row, tuple(jnp.zeros((SUB, lanes), F32) for _ in range(fields)), unroll=4
            )
            for f in range(fields):
                edge[f, pl.ds(pl.multiple_of(h * SUB, SUB), SUB), :] = acc[f]

        each(0, CH // SUB, sub)
        send_edges(0, c)

    def advance(t, c, last):
        for side in range(2):
            lon_copy(t, c, side).wait_recv()
            lat_copy(t, c, side).wait_recv()
        if not last:
            wait_w(c, 2)
            wait_w(c, 3)
        lane16 = lax.broadcasted_iota(jnp.int32, (CH, lanes), 1)
        for f in range(fields):
            from_west = lon_in[t, c, 0, f].astype(F32)
            from_east = lon_in[t, c, 1, f].astype(F32)
            ring[f] = jnp.where(
                lane16 % 2 == 1, pltpu.roll(from_west, 1, 1), pltpu.roll(from_east, lanes - 1, 1)
            )
            halo[0, f] = jnp.where(lat == 0, 0.0, lat_in[t, c, 0, f].astype(F32))
            halo[1, f] = jnp.where(lat == n_lat - 1, 0.0, lat_in[t, c, 1, f].astype(F32))

        def sub(h):
            low = pl.multiple_of(c * CH + h * SUB, SUB)
            inner = pl.ds(pl.multiple_of(h * SUB, SUB), SUB)
            k = [[coef[e, f, pl.ds(low, SUB), :] for f in range(fields)] for e in range(fields)]
            rims = [ring[f, inner, :] for f in range(fields)]

            def row(i, below, mid, above, acc):
                g = [cells[i, at(f, low), :] for f in range(fields)]
                u = winds[2 * t, i, pl.ds(low, SUB), :]
                back = lanes - 1 - 2 * i
                fresh = []
                for f in range(fields):
                    p = u * g[f]
                    rim = pltpu.roll(rims[f], back, 1)
                    from_west = jnp.where(lane == 0, rim, pltpu.roll(p, 1, 1))
                    from_east = jnp.where(lane == lanes - 1, rim, pltpu.roll(p, lanes - 1, 1))
                    total = k[0][f] * g[0]
                    for e in range(1, fields):
                        total = total + k[e][f] * g[e]
                    total = total - (from_west - from_east) - (below[f] - above[f])
                    cells[i, at(f, low), :] = total
                    fresh.append(total)
                if last:
                    return acc
                v = winds[2, i, pl.ds(low, SUB), :]
                here = pair == i
                return tuple(
                    jnp.where(here, pltpu.roll(v * fresh[f], 2 * i + 1, 1), acc[f])
                    for f in range(fields)
                )

            def lat_product(i):
                w = winds[2 * t + 1, i, pl.ds(low, SUB), :]
                return tuple(w * cells[i, at(f, low), :] for f in range(fields))

            def step(i, carry):
                below, mid, acc = carry
                above = lat_product(i + 1)
                acc = row(i, below, mid, above, acc)
                return mid, above, acc

            acc = () if last else tuple(jnp.zeros((SUB, lanes), F32) for _ in range(fields))
            below = tuple(halo[0, f, inner, :] for f in range(fields))
            below, mid, acc = lax.fori_loop(
                0, rows - 1, step, (below, lat_product(0), acc), unroll=3
            )
            above = tuple(halo[1, f, inner, :] for f in range(fields))
            acc = row(rows - 1, below, mid, above, acc)
            if not last:
                for f in range(fields):
                    edge[f, inner, :] = acc[f]

        each(0, CH // SUB, sub)
        if not last:
            send_edges(1, c)

    for e in range(fields):
        block = lim_ref[:, e, :]
        for f in range(fields):
            column = block[:, f : f + 1] + (1.0 if e == f else 0.0)
            coef[e, f] = jnp.broadcast_to(column, (levels, lanes))

    at_row = lax.broadcasted_iota(jnp.int32, (lanes, 2 * lanes), 0)
    at_col = lax.broadcasted_iota(jnp.int32, (lanes, 2 * lanes), 1)
    eye2[...] = jnp.where(at_row == at_col % lanes, 1.0, 0.0).astype(BF16)

    each(1, n_lon, lambda d: m_copy(d).start())
    own_m.start()
    each(0, chunks, first_edges)
    each(0, chunks, lambda c: advance(0, c, False))

    def finish(c):
        advance(1, c, True)

        def put(h):
            l = c * CH + h
            for f in range(fields):
                pltpu.make_async_copy(
                    cells.at[:, f * levels + l, :], a_ref.at[f, l], a_sem.at[c, f]
                ).start()

        each(0, CH, put)

    each(0, chunks, finish)

    def turn(i):
        x = cells[i]
        hi = x.astype(BF16)
        lo = (x - hi.astype(F32)).astype(BF16)
        both = jnp.concatenate([hi, lo], axis=1)
        r = lax.dot_general(
            eye2[...], both, (((1,), (1,)), ((), ())), preferred_element_type=F32
        )
        span = pl.ds(pl.multiple_of(i * lanes, lanes), lanes)
        columns[0, span, :] = r[:, :lanes]
        columns[1, span, : chan - lanes] = r[:, lanes:]

    each(0, rows, turn)

    each(1, n_lon, lambda d: slot_copy(d).wait_recv())
    own_slot.wait()
    to_sm = pltpu.make_async_copy(slot_in, slot_sm, local_sem.at[0])
    to_sm.start()
    to_sm.wait()

    def pick(d):
        def some(b):
            for j in range(16):
                n = b * 16 + j
                c = slot_sm[d, 0, n]
                to = d * slots + n
                picked[0, pl.ds(to, 1), :] = columns[0, pl.ds(c, 1), :]
                picked[1, pl.ds(to, 1), :] = columns[1, pl.ds(c, 1), :]

        each(0, slots // 16, some)

    each(0, n_lon, pick)

    eye = lax.broadcasted_iota(jnp.int32, (lanes, lanes), 0) == lax.broadcasted_iota(
        jnp.int32, (lanes, lanes), 1
    )

    def sens_copy(d):
        back = lax.rem(lon + n_lon - d, n_lon)
        return pltpu.make_async_remote_copy(
            src_ref=sens.at[d], dst_ref=sens_in.at[lon],
            send_sem=sens_send.at[d], recv_sem=sens_recv.at[d],
            device_id={"lon": back}, device_id_type=MESH,
        )

    def contract(d):
        for h in range(slots // lanes):
            span = pl.ds(pl.multiple_of(d * slots + h * lanes, lanes), lanes)
            x = jnp.concatenate(
                [picked[0, span, :], picked[1, span, : chan - lanes]], axis=1
            )
            hi = x.astype(BF16)
            lo = (x - hi.astype(F32)).astype(BF16)
            m = m_in[d, :, h * lanes : (h + 1) * lanes]
            r = jnp.dot(hi, m, preferred_element_type=F32) + jnp.dot(
                lo, m, preferred_element_type=F32
            )
            sens[d, :, h * lanes : (h + 1) * lanes] = jnp.sum(
                jnp.where(eye, r, 0.0), axis=0, keepdims=True
            )

    own_m.wait()
    contract(0)
    own_sens = pltpu.make_async_copy(sens.at[0], sens_in.at[lon], sens_recv.at[0])
    own_sens.start()

    def serve(d):
        m_copy(d).wait_recv()
        contract(d)
        sens_copy(d).start()

    each(1, n_lon, serve)

    own_sens.wait()
    each(1, n_lon, lambda d: sens_copy(d).wait_recv())
    s_ref[...] = sens_in[...]

    def drain(d):
        m_copy(d).wait_send()
        slot_copy(d).wait_send()
        sens_copy(d).wait_send()

    each(1, n_lon, drain)

    def drain_chunk(c):
        for t in range(2):
            for side in range(2):
                lon_copy(t, c, side).wait_send()
                lat_copy(t, c, side).wait_send()
        for f in range(fields):
            block = a_ref.at[f, pl.ds(c * CH, CH)]
            pltpu.make_async_copy(block, block, a_sem.at[c, f]).wait()

    each(0, chunks, drain_chunk)


def on_device(sizes, g, wind, lim, slot, tally, operator, departures):
    n_lon, n_lat = sizes
    fields, levels, rows, lanes = g.shape
    slots = slot.shape[2]
    chunks = levels // CH
    chan = fields * levels
    dims = (n_lon, n_lat, fields, levels, rows, lanes, slots)
    dma = pltpu.SemaphoreType.DMA
    anywhere = pl.BlockSpec(memory_space=pl.ANY)
    vmem = pl.BlockSpec(memory_space=pltpu.VMEM)
    analysis, sens = pl.pallas_call(
        functools.partial(kernel, dims),
        out_shape=(
            jax.ShapeDtypeStruct(g.shape, F32),
            jax.ShapeDtypeStruct((n_lon, 1, slots), F32),
        ),
        in_specs=[anywhere, anywhere, vmem, anywhere, anywhere],
        out_specs=(anywhere, vmem),
        scratch_shapes=[
            pltpu.VMEM((rows, chan, lanes), F32),
            pltpu.VMEM((4, rows, levels, lanes), F32),
            pltpu.VMEM((fields, fields, levels, lanes), F32),
            pltpu.VMEM((2, rows * lanes, lanes), F32),
            pltpu.VMEM((n_lon, chan, slots), BF16),
            pltpu.VMEM((n_lon, 1, slots), jnp.int32),
            pltpu.SMEM((n_lon, 1, slots), jnp.int32),
            pltpu.VMEM((2, n_lon * slots, lanes), F32),
            pltpu.VMEM((lanes, 2 * lanes), BF16),
            pltpu.VMEM((2, chunks, fields, CH, lanes), BF16),
            pltpu.VMEM((2, chunks, 2, fields, CH, lanes), BF16),
            pltpu.VMEM((2, chunks, 2, fields, CH, lanes), BF16),
            pltpu.VMEM((2, chunks, 2, fields, CH, lanes), BF16),
            pltpu.VMEM((fields, CH, lanes), F32),
            pltpu.VMEM((fields, CH, lanes), F32),
            pltpu.VMEM((2, fields, CH, lanes), F32),
            pltpu.VMEM((n_lon, 1, slots), F32),
            pltpu.VMEM((n_lon, 1, slots), F32),
            dma((chunks, fields)),
            dma((chunks, 4)),
            dma((chunks, fields)),
            dma((n_lon,)),
            dma((n_lon,)),
            dma((n_lon,)),
            dma((n_lon,)),
            dma((1,)),
            dma((2, chunks, 2)),
            dma((2, chunks, 2)),
            dma((2, chunks, 2)),
            dma((2, chunks, 2)),
            dma((n_lon,)),
            dma((n_lon,)),
        ],
        compiler_params=pltpu.CompilerParams(
            collective_id=0, has_side_effects=True, vmem_limit_bytes=58 << 20
        ),
    )(g, wind, lim, slot, operator)
    live = lax.broadcasted_iota(jnp.int32, (n_lon, slots), 1) < tally[0][:, None]
    impact = jnp.where(live, departures[0] * sens[:, 0], jnp.float32(0.0))[None]
    return analysis, impact


def solution(mesh):
    in_specs = (
        P(None, None, "lat", "lon"),
        P(None, None, None, "lat", "lon"),
        P(),
        P(("lon", "lat"), None, None),
        P(("lon", "lat"), None),
        P(("lon", "lat"), None, None, None),
        P(("lon", "lat"), None, None),
    )
    out_specs = (P(None, None, "lat", "lon"), P(("lon", "lat"), None, None))
    sizes = (mesh.shape["lon"], mesh.shape["lat"])
    return jax.shard_map(
        functools.partial(on_device, sizes),
        mesh=mesh, in_specs=in_specs, out_specs=out_specs, check_vma=False,
    )
```

time: 475 us -> 116 us (0.24); the launches traced: 466 us -> 116 us
  local copies, waits for them, and re-layouts: 283 us -> 8.67 us
  Pallas kernels: 0 us -> 105 us
  matrix products: 66 us -> 0 us
  other arithmetic: 47 us -> 0.8 us
  blocking collectives: 43.5 us -> 0 us
  starting transfers between devices: 25.2 us -> 0 us
    slice x18 -> x0, local copies, waits for them, and re-layouts: 132 us -> none  [the longest x4 39.5 us: on_device(): lon_edges = jnp.concatenate([lon_prod[..., :1], lon_prod[..., -1:]], axis=3)]
    pallas_call x0 -> x1, Pallas kernels: none -> 105 us  [on_device(): pl.pallas_call(functools.partial(kernel, dims), out_shape=(jax.ShapeDtype...]
    broadcast_in_dim x4 -> x0, local copies, waits for them, and re-layouts: 84.2 us -> none  [the longest x2 42.2 us: neighbour_terms(): jnp.where(position == 0, lower_rim, jnp.roll(product, 1, axis=axis))]
    dot_general x2 -> x0, matrix products: 66 us -> none  [couple(): jnp.einsum('lef,elab->flab', layer_interaction_matrix, prognostic_variabl...]
    all_to_all x1 -> x0, blocking collectives: 43.5 us -> none  [on_device(): lax.all_to_all(picked, 'lon', split_axis=1, concat_axis=1, tiled=True)]
    convert_element_type x2 -> x0, other arithmetic: 25 us -> none  [on_device(): extended(lon_edges.astype(jnp.bfloat16), (('lon', 3),), 1, True)]
    gather x2 -> x0, local copies, waits for them, and re-layouts: 23.3 us -> none  [on_device(): picked = flat[:, wanted]]
    ppermute x4 -> x0, local copies, waits for them, and re-layouts: 19.5 us -> none  [the longest x2 9.86 us: extended(): lax.ppermute(tail, axis, [(i, (i + 1) % count) for i in range(ends)])]
  transfers between devices with their start and end apart: 9 -> 0, of which waited for: 0 -> 0; matrix products, arithmetic and copies ran while one was open for 44% -> 0% of each run, Pallas kernels for 0% -> 0%
where the time goes in v1:
time: 116 us
  Pallas kernels  105 us (91%)
  local copies, waits for them, and re-layouts  8.67 us (7%)
    pallas_call x1, Pallas kernels, on_device(): pl.pallas_call(functools.partial(kernel, dims), out_shape=(jax.ShapeDtype...  105 us
    unnamed x7, local copies, waits for them, and re-layouts  8.67 us

profile of v1, /device:TPU:1, one launch (start us, length us, event | category | flops | bytes accessed | tf_op | source)
XLA Modules:
  0.0 115.5 jit_solution(12476583975223301829)
XLA Ops:
  0.6 1.4 %copy.9.lim_ref = f32[48,4,4]{2,1,0:T(4,128)} copy(f32[48,4,4]{0,2,1:T(4,128)} %param.9) | data formatting | bytes 6144 | tf_op args[2]
  2.1 0.0 copy-start
  2.1 0.0 copy-start.1
  2.1 105.4 %shard_map.89 = (f32[4,48,64,128]{3,2,1,0:T(8,128)}, f32[16,1,256]{2,1,0:T(1,128)}) custom-call(f32[4,48,64,128]{3,2,1,0:T(8,128)} %g_ref.1, f32[2,2,48,64,128]{4,3,2,1,0:T(8,128)} %wind_ref.1, f32[48,4,4]{2,1,0:T(4,128)} %copy.9.lim_ref, s32[1,16,256]{2,1,0:T(8,128)} %slot_ref.1, bf16[1,16,192,256]{3,2,1,0:T(8,128)(2,1)} %m_ref.1), custom_call_target="tpu_custom_call" | custom-call | tf_op jit(solution)/shard_map/pallas_call | solution.py:372
  107.5 0.0 copy-done
  107.5 0.0 copy-done.1
  107.5 0.8 compare_select_fusion
  108.3 0.6 copy.11
  108.9 6.6 %copy.14 = f32[4,48,64,128]{3,2,1,0:T(8,128)} copy(f32[4,48,64,128]{3,2,1,0:T(8,128)} %get-tuple-element.10) | data formatting | bytes 12582912
Async XLA Ops:
  2.1 105.4 %copy-start = (f32[1,16,256]{2,1,0:T(8,128)S(1)}, f32[1,16,256]{2,1,0:T(8,128)}, u32[]{:S(2)}) copy-start(f32[1,16,256]{2,1,0:T(8,128)} %param.13) | copy-start | bytes 49156
  2.1 105.4 %copy-start.1 = (s32[1,16]{1,0:T(1,128)S(1)}, s32[1,16]{1,0:T(1,128)}, u32[]{:S(2)}) copy-start(s32[1,16]{1,0:T(1,128)} %param.11) | copy-start | bytes 196

commit v2 on v1

--- a/solution.py
+++ b/solution.py
@@ -12,6 +12,7 @@
 BF16 = jnp.bfloat16
 CH = 16
 SUB = 8
+GR = 8
 
 
 def each(lo, hi, body, unroll=1):
@@ -26,8 +27,8 @@
     dims,
     g_ref, wind_ref, lim_ref, slot_ref, m_ref,
     a_ref, s_ref,
-    cells, winds, coef, columns, m_in, slot_in, slot_sm, picked, eye2,
-    lon_out, lon_in, lat_out, lat_in, edge, ring, halo, sens, sens_in,
+    cells, winds, coef, columns, m_in, slot_in, slot_sm, picked, eye2, shift,
+    lon_out, lon_in, lat_out, lat_in, halo, sens, sens_in,
     g_sem, w_sem, a_sem, m_send, m_recv, slot_send, slot_recv, local_sem,
     lon_send, lon_recv, lat_send, lat_recv, sens_send, sens_recv,
 ):
@@ -79,7 +80,6 @@
     each(1, n_lon, greet)
     for other in (north, south):
         pl.semaphore_signal(barrier, inc=1, device_id={"lat": other}, device_id_type=MESH)
-    pl.semaphore_wait(barrier, n_lon - 1 + 2)
 
     def slot_copy(d):
         peer = lax.rem(lon + d, n_lon)
@@ -101,9 +101,6 @@
         slot_ref.at[0, pl.ds(lon, 1), :], slot_in.at[0], slot_recv.at[0]
     )
     own_m = pltpu.make_async_copy(m_ref.at[0, lon], m_in.at[0], m_recv.at[0])
-    each(1, n_lon, lambda d: slot_copy(d).start())
-    own_slot.start()
-
     def lon_copy(t, c, side):
         return pltpu.make_async_remote_copy(
             src_ref=lon_out.at[t, c], dst_ref=lon_in.at[t, c, side],
@@ -118,20 +115,32 @@
             device_id={"lat": north if side == 0 else south}, device_id_type=MESH,
         )
 
-    lane = lax.broadcasted_iota(jnp.int32, (SUB, lanes), 1)
-    pair = lane // 2
-
     def at(f, low):
         return pl.ds(pl.multiple_of(f * levels + low, SUB), SUB)
 
-    def send_edges(t, c):
-        lon_out[t, c] = edge[...].astype(BF16)
+    def tag(shape, r0, c0, r1, c1, v0, v1):
+        r = lax.broadcasted_iota(jnp.int32, shape, 0)
+        c = lax.broadcasted_iota(jnp.int32, shape, 1)
+        first = jnp.where((r == r0) & (c == c0), v0, 0.0)
+        return (first + jnp.where((r == r1) & (c == c1), v1, 0.0)).astype(BF16)
+
+    groups = rows // GR
+
+    def rim_rows(q, b):
+        mask = tag((2 * groups, lanes), 2 * b, 0, 2 * b + 1, lanes - 1, 1.0, 1.0)
+        return lax.dot_general(
+            mask, q.astype(BF16), (((1,), (1,)), ((), ())), preferred_element_type=F32
+        )
+
+    def lat_edges(t, c):
         for side, row in ((0, rows - 1), (1, 0)):
             w = winds[2 * t + 1, row, pl.ds(c * CH, CH), :]
             for f in range(fields):
                 lat_out[t, c, side, f] = (
                     w * cells[row, pl.ds(f * levels + c * CH, CH), :]
                 ).astype(BF16)
+
+    def send_edges(t, c):
         for side in range(2):
             lon_copy(t, c, side).start()
             lat_copy(t, c, side).start()
@@ -140,26 +149,23 @@
         wait_g(c)
         wait_w(c, 0)
         wait_w(c, 1)
-
-        def sub(h):
+        for h in range(CH // SUB):
             low = pl.multiple_of(c * CH + h * SUB, SUB)
 
-            def row(i, acc):
-                u = winds[0, i, pl.ds(low, SUB), :]
-                here = pair == i
-                return tuple(
-                    jnp.where(here, pltpu.roll(u * cells[i, at(f, low), :], 2 * i + 1, 1), acc[f])
-                    for f in range(fields)
-                )
+            def group(b, acc):
+                parts = []
+                for r in range(GR):
+                    i = b * GR + r
+                    u = winds[0, i, pl.ds(low, SUB), :]
+                    parts += [u * cells[i, at(f, low), :] for f in range(fields)]
+                return acc + rim_rows(jnp.concatenate(parts, axis=0), b)
 
             acc = lax.fori_loop(
-                0, rows, row, tuple(jnp.zeros((SUB, lanes), F32) for _ in range(fields)), unroll=4
-            )
-            for f in range(fields):
-                edge[f, pl.ds(pl.multiple_of(h * SUB, SUB), SUB), :] = acc[f]
-
-        each(0, CH // SUB, sub)
-        send_edges(0, c)
+                0, groups, group,
+                jnp.zeros((2 * groups, GR * fields * SUB), F32), unroll=8,
+            )
+            lon_out[0, c, h] = acc.astype(BF16)
+        lat_edges(0, c)
 
     def advance(t, c, last):
         for side in range(2):
@@ -168,13 +174,7 @@
         if not last:
             wait_w(c, 2)
             wait_w(c, 3)
-        lane16 = lax.broadcasted_iota(jnp.int32, (CH, lanes), 1)
         for f in range(fields):
-            from_west = lon_in[t, c, 0, f].astype(F32)
-            from_east = lon_in[t, c, 1, f].astype(F32)
-            ring[f] = jnp.where(
-                lane16 % 2 == 1, pltpu.roll(from_west, 1, 1), pltpu.roll(from_east, lanes - 1, 1)
-            )
             halo[0, f] = jnp.where(lat == 0, 0.0, lat_in[t, c, 0, f].astype(F32))
             halo[1, f] = jnp.where(lat == n_lat - 1, 0.0, lat_in[t, c, 1, f].astype(F32))
 
@@ -182,72 +182,108 @@
             low = pl.multiple_of(c * CH + h * SUB, SUB)
             inner = pl.ds(pl.multiple_of(h * SUB, SUB), SUB)
             k = [[coef[e, f, pl.ds(low, SUB), :] for f in range(fields)] for e in range(fields)]
-            rims = [ring[f, inner, :] for f in range(fields)]
-
-            def row(i, below, mid, above, acc):
-                g = [cells[i, at(f, low), :] for f in range(fields)]
-                u = winds[2 * t, i, pl.ds(low, SUB), :]
-                back = lanes - 1 - 2 * i
-                fresh = []
-                for f in range(fields):
-                    p = u * g[f]
-                    rim = pltpu.roll(rims[f], back, 1)
-                    from_west = jnp.where(lane == 0, rim, pltpu.roll(p, 1, 1))
-                    from_east = jnp.where(lane == lanes - 1, rim, pltpu.roll(p, lanes - 1, 1))
-                    total = k[0][f] * g[0]
-                    for e in range(1, fields):
-                        total = total + k[e][f] * g[e]
-                    total = total - (from_west - from_east) - (below[f] - above[f])
-                    cells[i, at(f, low), :] = total
-                    fresh.append(total)
-                if last:
-                    return acc
-                v = winds[2, i, pl.ds(low, SUB), :]
-                here = pair == i
-                return tuple(
-                    jnp.where(here, pltpu.roll(v * fresh[f], 2 * i + 1, 1), acc[f])
-                    for f in range(fields)
-                )
+            both = jnp.concatenate([lon_in[t, c, 0, h], lon_in[t, c, 1, h]], axis=0)
+            rims = jnp.transpose(both.astype(F32)).astype(BF16)
 
             def lat_product(i):
                 w = winds[2 * t + 1, i, pl.ds(low, SUB), :]
-                return tuple(w * cells[i, at(f, low), :] for f in range(fields))
-
-            def step(i, carry):
+                return [w * cells[i, at(f, low), :] for f in range(fields)]
+
+            def group(b, carry):
                 below, mid, acc = carry
-                above = lat_product(i + 1)
-                acc = row(i, below, mid, above, acc)
-                return mid, above, acc
-
-            acc = () if last else tuple(jnp.zeros((SUB, lanes), F32) for _ in range(fields))
-            below = tuple(halo[0, f, inner, :] for f in range(fields))
+                base = b * GR
+                g = [[cells[base + r, at(f, low), :] for f in range(fields)] for r in range(GR)]
+                parts = []
+                for r in range(GR):
+                    u = winds[2 * t, base + r, pl.ds(low, SUB), :]
+                    parts += [u * g[r][f] for f in range(fields)]
+                p = jnp.concatenate(parts, axis=0)
+                hi = p.astype(BF16)
+                lo = (p - hi.astype(F32)).astype(BF16)
+                place = tag(
+                    (4 * groups, lanes), 2 * b + 1, 0, 2 * groups + 2 * b, lanes - 1, -1.0, 1.0
+                )
+                lon_term = jnp.dot(
+                    jnp.concatenate([hi, lo], axis=1), shift[...], preferred_element_type=F32
+                ) + jnp.dot(rims, place, preferred_element_type=F32)
+                fresh = []
+                for r in range(GR):
+                    if r < GR - 1:
+                        w = winds[2 * t + 1, base + r + 1, pl.ds(low, SUB), :]
+                        above = [w * g[r + 1][f] for f in range(fields)]
+                    else:
+                        over = b == groups - 1
+                        nxt = lat_product(jnp.minimum(base + GR, rows - 1))
+                        above = [
+                            jnp.where(over, halo[1, f, inner, :], nxt[f]) for f in range(fields)
+                        ]
+                    for f in range(fields):
+                        total = k[0][f] * g[r][0]
+                        for e in range(1, fields):
+                            total = total + k[e][f] * g[r][e]
+                        n = (r * fields + f) * SUB
+                        total = total + (above[f] - below[f]) + lon_term[n : n + SUB]
+                        cells[base + r, at(f, low), :] = total
+                        fresh.append(total)
+                    below, mid = mid, above
+                if not last:
+                    parts = []
+                    for r in range(GR):
+                        v = winds[2, base + r, pl.ds(low, SUB), :]
+                        parts += [v * fresh[r * fields + f] for f in range(fields)]
+                    acc = acc + rim_rows(jnp.concatenate(parts, axis=0), b)
+                return below, mid, acc
+
+            acc = () if last else jnp.zeros((2 * groups, GR * fields * SUB), F32)
+            below = [halo[0, f, inner, :] for f in range(fields)]
             below, mid, acc = lax.fori_loop(
-                0, rows - 1, step, (below, lat_product(0), acc), unroll=3
-            )
-            above = tuple(halo[1, f, inner, :] for f in range(fields))
-            acc = row(rows - 1, below, mid, above, acc)
+                0, groups, group, (below, lat_product(0), acc), unroll=4
+            )
             if not last:
-                for f in range(fields):
-                    edge[f, inner, :] = acc[f]
+                lon_out[1, c, h] = acc.astype(BF16)
 
         each(0, CH // SUB, sub)
         if not last:
+            lat_edges(1, c)
             send_edges(1, c)
 
+    diag = lax.broadcasted_iota(jnp.int32, (levels, levels), 0) == lax.broadcasted_iota(
+        jnp.int32, (levels, levels), 1
+    )
     for e in range(fields):
-        block = lim_ref[:, e, :]
         for f in range(fields):
-            column = block[:, f : f + 1] + (1.0 if e == f else 0.0)
+            line = lim_ref[e, f : f + 1, :] + (1.0 if e == f else 0.0)
+            column = jnp.sum(
+                jnp.where(diag, jnp.broadcast_to(line, (levels, levels)), 0.0),
+                axis=1, keepdims=True,
+            )
             coef[e, f] = jnp.broadcast_to(column, (levels, lanes))
 
     at_row = lax.broadcasted_iota(jnp.int32, (lanes, 2 * lanes), 0)
     at_col = lax.broadcasted_iota(jnp.int32, (lanes, 2 * lanes), 1)
     eye2[...] = jnp.where(at_row == at_col % lanes, 1.0, 0.0).astype(BF16)
-
-    each(1, n_lon, lambda d: m_copy(d).start())
+    to_row = lax.broadcasted_iota(jnp.int32, (2 * lanes, lanes), 0) % lanes
+    to_col = lax.broadcasted_iota(jnp.int32, (2 * lanes, lanes), 1)
+    shift[...] = (
+        jnp.where(to_row == to_col + 1, 1.0, 0.0) - jnp.where(to_row == to_col - 1, 1.0, 0.0)
+    ).astype(BF16)
+
+    each(0, chunks, first_edges)
+    pl.semaphore_wait(barrier, n_lon - 1 + 2)
+    each(0, chunks, lambda c: send_edges(0, c))
+    each(1, n_lon, lambda d: slot_copy(d).start())
+    own_slot.start()
     own_m.start()
-    each(0, chunks, first_edges)
-    each(0, chunks, lambda c: advance(0, c, False))
+    share = (n_lon - 1) // (chunks + 1)
+    head = n_lon - chunks * (share + 1)
+    each(1, head, lambda d: m_copy(d).start())
+
+    def begin(c):
+        advance(0, c, False)
+        low = head + c * (share + 1)
+        each(low, low + share + 1, lambda d: m_copy(d).start())
+
+    each(0, chunks, begin)
 
     def finish(c):
         advance(1, c, True)
@@ -262,6 +298,9 @@
         each(0, CH, put)
 
     each(0, chunks, finish)
+
+    flat = columns.reshape(2, rows * lanes, lanes)
+    taken = picked.reshape(2, n_lon * slots, lanes)
 
     def turn(i):
         x = cells[i]
@@ -272,10 +311,10 @@
             eye2[...], both, (((1,), (1,)), ((), ())), preferred_element_type=F32
         )
         span = pl.ds(pl.multiple_of(i * lanes, lanes), lanes)
-        columns[0, span, :] = r[:, :lanes]
-        columns[1, span, : chan - lanes] = r[:, lanes:]
-
-    each(0, rows, turn)
+        flat[0, span, :] = r[:, :lanes]
+        flat[1, span, : chan - lanes] = r[:, lanes:]
+
+    each(0, rows, turn, unroll=4)
 
     each(1, n_lon, lambda d: slot_copy(d).wait_recv())
     own_slot.wait()
@@ -285,12 +324,11 @@
 
     def pick(d):
         def some(b):
+            cs = [slot_sm[d, 0, b * 16 + j] for j in range(16)]
+            parts = [(columns[0, c], columns[1, c]) for c in cs]
             for j in range(16):
-                n = b * 16 + j
-                c = slot_sm[d, 0, n]
-                to = d * slots + n
-                picked[0, pl.ds(to, 1), :] = columns[0, pl.ds(c, 1), :]
-                picked[1, pl.ds(to, 1), :] = columns[1, pl.ds(c, 1), :]
+                for q in range(2):
+                    picked[q, d * slots + b * 16 + j] = parts[j][q]
 
         each(0, slots // 16, some)
 
@@ -312,7 +350,7 @@
         for h in range(slots // lanes):
             span = pl.ds(pl.multiple_of(d * slots + h * lanes, lanes), lanes)
             x = jnp.concatenate(
-                [picked[0, span, :], picked[1, span, : chan - lanes]], axis=1
+                [taken[0, span, :], taken[1, span, : chan - lanes]], axis=1
             )
             hi = x.astype(BF16)
             lo = (x - hi.astype(F32)).astype(BF16)
@@ -325,20 +363,15 @@
             )
 
     own_m.wait()
-    contract(0)
+    each(1, n_lon, lambda d: m_copy(d).wait_recv())
+    each(0, n_lon, contract, unroll=4)
+    each(1, n_lon, lambda d: sens_copy(d).start())
     own_sens = pltpu.make_async_copy(sens.at[0], sens_in.at[lon], sens_recv.at[0])
     own_sens.start()
 
-    def serve(d):
-        m_copy(d).wait_recv()
-        contract(d)
-        sens_copy(d).start()
-
-    each(1, n_lon, serve)
-
     own_sens.wait()
     each(1, n_lon, lambda d: sens_copy(d).wait_recv())
-    s_ref[...] = sens_in[...]
+    s_ref[...] = sens_in[:, 0, :]
 
     def drain(d):
         m_copy(d).wait_send()
@@ -357,6 +390,13 @@
             pltpu.make_async_copy(block, block, a_sem.at[c, f]).wait()
 
     each(0, chunks, drain_chunk)
+
+
+def hand_over(from_ref, to_ref, sem):
+    for f in range(from_ref.shape[0]):
+        pltpu.make_async_copy(from_ref.at[f], to_ref.at[f], sem.at[f]).start()
+    for f in range(from_ref.shape[0]):
+        pltpu.make_async_copy(from_ref.at[f], to_ref.at[f], sem.at[f]).wait()
 
 
 def on_device(sizes, g, wind, lim, slot, tally, operator, departures):
@@ -372,27 +412,26 @@
     analysis, sens = pl.pallas_call(
         functools.partial(kernel, dims),
         out_shape=(
-            jax.ShapeDtypeStruct(g.shape, F32),
-            jax.ShapeDtypeStruct((n_lon, 1, slots), F32),
+            pltpu.VMEM(g.shape, F32),
+            jax.ShapeDtypeStruct((n_lon, slots), F32),
         ),
         in_specs=[anywhere, anywhere, vmem, anywhere, anywhere],
-        out_specs=(anywhere, vmem),
+        out_specs=(vmem, vmem),
         scratch_shapes=[
             pltpu.VMEM((rows, chan, lanes), F32),
             pltpu.VMEM((4, rows, levels, lanes), F32),
             pltpu.VMEM((fields, fields, levels, lanes), F32),
-            pltpu.VMEM((2, rows * lanes, lanes), F32),
+            pltpu.VMEM((2, rows * lanes, 1, lanes), F32),
             pltpu.VMEM((n_lon, chan, slots), BF16),
             pltpu.VMEM((n_lon, 1, slots), jnp.int32),
             pltpu.SMEM((n_lon, 1, slots), jnp.int32),
-            pltpu.VMEM((2, n_lon * slots, lanes), F32),
+            pltpu.VMEM((2, n_lon * slots, 1, lanes), F32),
             pltpu.VMEM((lanes, 2 * lanes), BF16),
-            pltpu.VMEM((2, chunks, fields, CH, lanes), BF16),
+            pltpu.VMEM((2 * lanes, lanes), BF16),
+            pltpu.VMEM((2, chunks, CH // SUB, 2 * rows // GR, GR * fields * SUB), BF16),
+            pltpu.VMEM((2, chunks, 2, CH // SUB, 2 * rows // GR, GR * fields * SUB), BF16),
             pltpu.VMEM((2, chunks, 2, fields, CH, lanes), BF16),
             pltpu.VMEM((2, chunks, 2, fields, CH, lanes), BF16),
-            pltpu.VMEM((2, chunks, 2, fields, CH, lanes), BF16),
-            pltpu.VMEM((fields, CH, lanes), F32),
-            pltpu.VMEM((fields, CH, lanes), F32),
             pltpu.VMEM((2, fields, CH, lanes), F32),
             pltpu.VMEM((n_lon, 1, slots), F32),
             pltpu.VMEM((n_lon, 1, slots), F32),
@@ -412,11 +451,18 @@
             dma((n_lon,)),
         ],
         compiler_params=pltpu.CompilerParams(
-            collective_id=0, has_side_effects=True, vmem_limit_bytes=58 << 20
+            collective_id=0, has_side_effects=True, vmem_limit_bytes=50 << 20
         ),
-    )(g, wind, lim, slot, operator)
+    )(g, wind, jnp.transpose(lim, (1, 2, 0)), slot, operator)
+    analysis = pl.pallas_call(
+        hand_over,
+        out_shape=jax.ShapeDtypeStruct(g.shape, F32),
+        in_specs=[vmem], out_specs=anywhere,
+        scratch_shapes=[dma((fields,))],
+        compiler_params=pltpu.CompilerParams(vmem_limit_bytes=1 << 20),
+    )(pltpu.with_memory_space_constraint(analysis, pltpu.VMEM))
     live = lax.broadcasted_iota(jnp.int32, (n_lon, slots), 1) < tally[0][:, None]
-    impact = jnp.where(live, departures[0] * sens[:, 0], jnp.float32(0.0))[None]
+    impact = jnp.where(live, departures[0] * sens, jnp.float32(0.0))[None]
     return analysis, impact
 
 

time: 116 us -> 77 us (0.66)
  Pallas kernels: 105 us -> 75.4 us
  local copies, waits for them, and re-layouts: 8.67 us -> 0.02 us
    pallas_call x1 -> x2, Pallas kernels: 105 us -> 75.4 us  [the longest x1 72.7 us: on_device(): pl.pallas_call(functools.partial(kernel, dims), out_shape=(pltpu.VMEM(g.s...]
    unnamed x7 -> x6, local copies, waits for them, and re-layouts: 8.67 us -> 0.02 us
where the time goes in v2:
time: 77 us; the launch traced here: 76.8 us
  Pallas kernels  75.4 us (98%)
    pallas_call x1, Pallas kernels, on_device(): pl.pallas_call(functools.partial(kernel, dims), out_shape=(pltpu.VMEM(g.s...  72.7 us
    pallas_call x1, Pallas kernels, on_device(): pl.pallas_call(hand_over, out_shape=jax.ShapeDtypeStruct(g.shape, F32), i...  2.73 us

profile of v2, /device:TPU:1, one launch (start us, length us, event | category | flops | bytes accessed | tf_op | source)
XLA Modules:
  0.0 76.8 jit_solution(4338398345554192208)
XLA Ops:
  0.6 72.7 %shard_map.86 = (f32[4,48,64,128]{3,2,1,0:T(8,128)S(1)}, f32[16,256]{1,0:T(8,128)}) custom-call(f32[4,48,64,128]{3,2,1,0:T(8,128)} %g_ref.1, f32[2,2,48,64,128]{4,3,2,1,0:T(8,128)} %wind_ref.1, f32[4,4,48]{2,1,0:T(4,128)} %bitcast.10, s32[1,16,256]{2,1,0:T(8,128)} %slot_ref.1, bf16[1,16,192,256]{3,2,1,0:T(8,128)(2,1)} %m_ref.1), custom_call_target="tpu_custom_call" | custom-call | tf_op jit(solution)/shard_map/pallas_call | solution.py:412
  73.3 0.0 copy-start
  73.3 0.0 copy-start.1
  73.3 0.0 copy-start.2
  73.4 2.7 %shard_map.87 = f32[4,48,64,128]{3,2,1,0:T(8,128)} custom-call(f32[4,48,64,128]{3,2,1,0:T(8,128)S(1)} %get-tuple-element.4.from_ref), custom_call_target="tpu_custom_call" | custom-call | tf_op jit(solution)/shard_map/pallas_call | solution.py:457
  76.1 0.0 copy-done
  76.1 0.0 copy-done.1
  76.1 0.0 copy-done.2
  76.1 0.7 fusion.1
Async XLA Ops:
  73.3 2.8 %copy-start = (f32[1,16,256]{2,1,0:T(8,128)S(1)}, f32[1,16,256]{2,1,0:T(8,128)}, u32[]{:S(2)}) copy-start(f32[1,16,256]{2,1,0:T(8,128)} %param.13) | copy-start | bytes 49156
  73.3 2.8 %copy-start.1 = (f32[16,256]{1,0:T(8,128)S(1)}, f32[16,256]{1,0:T(8,128)}, u32[]{:S(2)}) copy-start(f32[16,256]{1,0:T(8,128)} %get-tuple-element.5) | copy-start | bytes 49156
  73.3 2.8 %copy-start.2 = (s32[1,16]{1,0:T(1,128)S(1)}, s32[1,16]{1,0:T(1,128)}, u32[]{:S(2)}) copy-start(s32[1,16]{1,0:T(1,128)} %param.11) | copy-start | bytes 196

commit v3 on v2

--- a/solution.py
+++ b/solution.py
@@ -180,7 +180,7 @@
 
         def sub(h):
             low = pl.multiple_of(c * CH + h * SUB, SUB)
-            inner = pl.ds(pl.multiple_of(h * SUB, SUB), SUB)
+            inner = pl.ds(h * SUB, SUB)
             k = [[coef[e, f, pl.ds(low, SUB), :] for f in range(fields)] for e in range(fields)]
             both = jnp.concatenate([lon_in[t, c, 0, h], lon_in[t, c, 1, h]], axis=0)
             rims = jnp.transpose(both.astype(F32)).astype(BF16)
@@ -237,12 +237,13 @@
             acc = () if last else jnp.zeros((2 * groups, GR * fields * SUB), F32)
             below = [halo[0, f, inner, :] for f in range(fields)]
             below, mid, acc = lax.fori_loop(
-                0, groups, group, (below, lat_product(0), acc), unroll=4
+                0, groups, group, (below, lat_product(0), acc), unroll=8
             )
             if not last:
                 lon_out[1, c, h] = acc.astype(BF16)
 
-        each(0, CH // SUB, sub)
+        for h in range(CH // SUB):
+            sub(h)
         if not last:
             lat_edges(1, c)
             send_edges(1, c)
@@ -274,16 +275,12 @@
     each(1, n_lon, lambda d: slot_copy(d).start())
     own_slot.start()
     own_m.start()
-    share = (n_lon - 1) // (chunks + 1)
-    head = n_lon - chunks * (share + 1)
-    each(1, head, lambda d: m_copy(d).start())
 
     def begin(c):
         advance(0, c, False)
-        low = head + c * (share + 1)
-        each(low, low + share + 1, lambda d: m_copy(d).start())
 
     each(0, chunks, begin)
+    each(1, n_lon, lambda d: m_copy(d).start())
 
     def finish(c):
         advance(1, c, True)
@@ -297,6 +294,10 @@
 
         each(0, CH, put)
 
+    each(1, n_lon, lambda d: slot_copy(d).wait_recv())
+    own_slot.wait()
+    to_sm = pltpu.make_async_copy(slot_in, slot_sm, local_sem.at[0])
+    to_sm.start()
     each(0, chunks, finish)
 
     flat = columns.reshape(2, rows * lanes, lanes)
@@ -314,12 +315,8 @@
         flat[0, span, :] = r[:, :lanes]
         flat[1, span, : chan - lanes] = r[:, lanes:]
 
-    each(0, rows, turn, unroll=4)
-
-    each(1, n_lon, lambda d: slot_copy(d).wait_recv())
-    own_slot.wait()
-    to_sm = pltpu.make_async_copy(slot_in, slot_sm, local_sem.at[0])
-    to_sm.start()
+    each(0, rows, turn, unroll=8)
+
     to_sm.wait()
 
     def pick(d):
@@ -330,7 +327,7 @@
                 for q in range(2):
                     picked[q, d * slots + b * 16 + j] = parts[j][q]
 
-        each(0, slots // 16, some)
+        each(0, slots // 16, some, unroll=4)
 
     each(0, n_lon, pick)
 
@@ -363,9 +360,17 @@
             )
 
     own_m.wait()
-    each(1, n_lon, lambda d: m_copy(d).wait_recv())
-    each(0, n_lon, contract, unroll=4)
-    each(1, n_lon, lambda d: sens_copy(d).start())
+    contract(0)
+
+    def serve(q):
+        for j in range(3):
+            m_copy(3 * q + 1 + j).wait_recv()
+        for j in range(3):
+            contract(3 * q + 1 + j)
+        for j in range(3):
+            sens_copy(3 * q + 1 + j).start()
+
+    each(0, (n_lon - 1) // 3, serve)
     own_sens = pltpu.make_async_copy(sens.at[0], sens_in.at[lon], sens_recv.at[0])
     own_sens.start()
 

time: 77 us -> 66.8 us (0.87)
  Pallas kernels: 75.4 us -> 65.3 us
    pallas_call x1, Pallas kernels: 72.7 us -> 62.6 us  [on_device(): pl.pallas_call(functools.partial(kernel, dims), out_shape=(pltpu.VMEM(g.s...]
where the time goes in v3:
time: 66.8 us; the launch traced here: 66.7 us
  Pallas kernels  65.3 us (98%)
  between operations  0.69 us (1%)
  other arithmetic  0.68 us (1%)
    pallas_call x1, Pallas kernels, on_device(): pl.pallas_call(functools.partial(kernel, dims), out_shape=(pltpu.VMEM(g.s...  62.6 us
    pallas_call x1, Pallas kernels, on_device(): pl.pallas_call(hand_over, out_shape=jax.ShapeDtypeStruct(g.shape, F32), i...  2.73 us

profile of v3, /device:TPU:1, one launch (start us, length us, event | category | flops | bytes accessed | tf_op | source)
XLA Modules:
  0.0 66.7 jit_solution(2367565345880281288)
XLA Ops:
  0.6 62.6 %shard_map.86 = (f32[4,48,64,128]{3,2,1,0:T(8,128)S(1)}, f32[16,256]{1,0:T(8,128)}) custom-call(f32[4,48,64,128]{3,2,1,0:T(8,128)} %g_ref.1, f32[2,2,48,64,128]{4,3,2,1,0:T(8,128)} %wind_ref.1, f32[4,4,48]{2,1,0:T(4,128)} %bitcast.10, s32[1,16,256]{2,1,0:T(8,128)} %slot_ref.1, bf16[1,16,192,256]{3,2,1,0:T(8,128)(2,1)} %m_ref.1), custom_call_target="tpu_custom_call" | custom-call | tf_op jit(solution)/shard_map/pallas_call | solution.py:417
  63.2 0.0 copy-start
  63.2 0.0 copy-start.1
  63.2 0.0 copy-start.2
  63.2 2.7 %shard_map.87 = f32[4,48,64,128]{3,2,1,0:T(8,128)} custom-call(f32[4,48,64,128]{3,2,1,0:T(8,128)S(1)} %get-tuple-element.4.from_ref), custom_call_target="tpu_custom_call" | custom-call | tf_op jit(solution)/shard_map/pallas_call | solution.py:462
  66.0 0.0 copy-done
  66.0 0.0 copy-done.1
  66.0 0.0 copy-done.2
  66.0 0.7 %fusion.1 = f32[1,16,256]{2,1,0:T(8,128)} fusion(f32[16,256]{1,0:T(8,128)S(1)} %copy-done.1, f32[1,16,256]{2,1,0:T(8,128)S(1)} %copy-done, s32[16]{0:T(128)S(1)} %bitcast.11), kind=kLoop, calls=%fused_computation.2 | loop fusion | flops 12288 | bytes 49216 | tf_op jit(solution)/shard_map/broadcast_in_dim | solution.py:470
Async XLA Ops:
  63.2 2.8 %copy-start = (f32[1,16,256]{2,1,0:T(8,128)S(1)}, f32[1,16,256]{2,1,0:T(8,128)}, u32[]{:S(2)}) copy-start(f32[1,16,256]{2,1,0:T(8,128)} %param.13) | copy-start | bytes 49156
  63.2 2.8 %copy-start.1 = (f32[16,256]{1,0:T(8,128)S(1)}, f32[16,256]{1,0:T(8,128)}, u32[]{:S(2)}) copy-start(f32[16,256]{1,0:T(8,128)} %get-tuple-element.5) | copy-start | bytes 49156
  63.2 2.8 %copy-start.2 = (s32[1,16]{1,0:T(1,128)S(1)}, s32[1,16]{1,0:T(1,128)}, u32[]{:S(2)}) copy-start(s32[1,16]{1,0:T(1,128)} %param.11) | copy-start | bytes 196
